TPU v7x, 128 devices: a whole 4x4x4 slice. The times are simulated.
128 devices in a mesh: req: 16 (over x, y), row: 8 (over z, core).
Axes of the slice: x: 4, y: 4, z: 4, core: 2. Of those that a mesh axis runs over, the one named last changes fastest.
Arguments:
- patches: bfloat16 [8, 2048, 1280], P('row', 'req'), may hold values from -6 to 6
- picture_ids: int32 [8, 2048], P('row'), may hold values from -1 to 15, as said below
- ln_attn: float32 [1280], replicated, may hold values from 0.1 to 1.9
- w_qkv: bfloat16 [3, 1280, 1280], P(None, None, 'req'), may hold values from -6 to 6
- w_out: bfloat16 [1280, 1280], P('req'), may hold values from -1.25 to 1.25
- ln_mlp: float32 [1280], replicated, may hold values from 0.1 to 1.9
- w_up: bfloat16 [1280, 5120], P(None, 'req'), may hold values from -0.15625 to 0.15625
- w_down: bfloat16 [5120, 1280], P('req'), may hold values from -0.3125 to 0.3125
- w_merge: bfloat16 [5120, 1280], replicated, may hold values from -0.078125 to 0.078125
- text_embed: bfloat16 [16384, 1280], P(('req', 'row')), may hold values from -6 to 6
- slot_dest: int32 [8, 512], P('row', 'req'), may hold values from -1 to 16383, as said below
Outputs:
- prompt_embed: bfloat16 [16384, 1280], P(('req', 'row'))
Inputs may be any that keep to these rules, and one draw needn't show every extreme that they name: `picture_ids`: each group holds whole pictures one after another from its first row, each picture's length a multiple of 4 and laid out so that every aligned run of four rows is one 2x2 window; rows after the last picture are padding. `slot_dest`: A merged row has a prompt row exactly when its patch rows belong to a picture; no prompt row is named twice; a merged row of group g (rows of the row index g) names a prompt row of a device with the same row index; at most 2 merged rows of one device name prompt rows of one device, and in every draw some device sends that many to one device.
All inputs are finite; a program needn't handle non-finite values.
Results may differ from a plain program's by a relative error of at most 0.023.
Values may be sent and summed in bfloat16 or wider, within the bound.
No kernel may reach another device: no remote copies, remote signals or barrier semaphores. Data moves between devices by JAX's collectives and lax.ppermute only.
A program may use at most 128 MiB of HBM per device.

v0:
```python
import math
import jax
import jax.numpy as jnp
from jax import lax
from jax.sharding import PartitionSpec as P

HEAD = 80


def layer_norm(rows, gain):
    rows32 = rows.astype(jnp.float32)
    center = rows32 - jnp.mean(rows32, axis=-1, keepdims=True)
    spread = jnp.mean(center * center, axis=-1, keepdims=True)
    return center * lax.rsqrt(spread + 1e-06) * gain


def local(
    patches,
    picture_ids,
    ln_attn,
    w_qkv,
    w_out,
    ln_mlp,
    w_up,
    w_down,
    w_merge,
    text_embed,
    slot_dest,
):
    rows = patches[0]
    local_rows = rows.shape[0]
    width = rows.shape[1]
    ids = picture_ids[0]
    group_rows = ids.shape[0]
    head_cols = w_out.shape[0]
    req_count = lax.axis_size("req")
    row_count = lax.axis_size("row")
    normed = layer_norm(rows, ln_attn).astype(jnp.bfloat16)
    qkv = jnp.einsum(
        "rd,tdc->trc",
        lax.all_gather(normed, "req", axis=0, tiled=True),
        w_qkv,
        preferred_element_type=jnp.float32,
    ).astype(jnp.bfloat16)
    keys = qkv[1]
    values = qkv[2]
    block = min(512, group_rows)
    blocks = group_rows // block
    scale = 1.0 / math.sqrt(HEAD)

    def attend(item):
        query_block, id_block = item
        same = id_block[:, None] == ids[None, :]
        scores = (
            jnp.einsum("qc,kc->qk", query_block, keys, preferred_element_type=jnp.float32) * scale
        )
        scores = jnp.where(same, scores, -1e30)
        top = jnp.max(scores, axis=1, keepdims=True)
        expo = jnp.exp(scores - top)
        probs = (expo / jnp.sum(expo, axis=1, keepdims=True)).astype(jnp.bfloat16)
        results = [jnp.dot(probs, values, preferred_element_type=jnp.float32).astype(jnp.bfloat16)]
        return jnp.concatenate(results, axis=1)

    attended = lax.map(
        attend, (qkv[0].reshape(blocks, block, head_cols), ids.reshape(blocks, block))
    )
    attended = attended.reshape(group_rows, head_cols)
    piece = lax.slice_in_dim(attended, 0, local_rows * lax.axis_size("req"), axis=0)
    attn = lax.psum_scatter(
        jnp.dot(piece, w_out, preferred_element_type=jnp.float32).astype(jnp.bfloat16),
        "req",
        scatter_dimension=0,
        tiled=True,
    ).astype(jnp.float32)
    resid = (rows.astype(jnp.float32) + attn).astype(jnp.bfloat16)
    normed_two = layer_norm(resid, ln_mlp).astype(jnp.bfloat16)
    hidden = jax.nn.gelu(
        jnp.dot(
            lax.all_gather(normed_two, "req", axis=0, tiled=True),
            w_up,
            preferred_element_type=jnp.float32,
        ),
        approximate=False,
    ).astype(jnp.bfloat16)
    piece = lax.slice_in_dim(hidden, 0, local_rows * lax.axis_size("req"), axis=0)
    mlp = lax.psum_scatter(
        jnp.dot(piece, w_down, preferred_element_type=jnp.float32).astype(jnp.bfloat16),
        "req",
        scatter_dimension=0,
        tiled=True,
    ).astype(jnp.float32)
    vision = (resid.astype(jnp.float32) + mlp).astype(jnp.bfloat16)
    merged = vision.reshape(local_rows // 4, 4 * width)
    merged_count = merged.shape[0]
    dest = slot_dest[0]
    prompt_rows = text_embed.shape[0]
    slot_cap = max(2, merged_count // req_count)
    owner = jnp.where(dest >= 0, dest // prompt_rows // row_count, -1)
    order = jnp.arange(merged_count)
    same_owner = (owner[:, None] == owner[None, :]) & (order[None, :] < order[:, None])
    ranks = jnp.sum(same_owner.astype(jnp.int32), axis=1)
    target = jnp.where(owner >= 0, owner * slot_cap + ranks, -1)
    select = target[None, :] == jnp.arange(req_count * slot_cap)[:, None]
    places = jnp.sum(jnp.where(select, (dest % prompt_rows + 1)[None, :], 0), axis=1) - 1
    chooser = select.astype(jnp.bfloat16)
    outgoing = jnp.dot(chooser, merged, preferred_element_type=jnp.float32).astype(jnp.bfloat16)
    arrived, landing = (
        lax.all_to_all(
            outgoing.reshape(req_count, slot_cap, -1),
            "req",
            split_axis=0,
            concat_axis=0,
            tiled=True,
        ),
        lax.all_to_all(
            places.reshape(req_count, slot_cap), "req", split_axis=0, concat_axis=0, tiled=True
        ),
    )
    arrived = arrived.reshape(req_count * slot_cap, -1)
    landing = landing.reshape(-1)
    incoming = jnp.dot(arrived, w_merge, preferred_element_type=jnp.float32).astype(jnp.bfloat16)
    placer = landing[None, :] == jnp.arange(prompt_rows)[:, None]
    placed = jnp.dot(
        placer.astype(jnp.bfloat16), incoming, preferred_element_type=jnp.float32
    ).astype(jnp.bfloat16)
    filled = jnp.any(placer, axis=1)
    return jnp.where(filled[:, None], placed, text_embed)


def solution(mesh):
    return jax.shard_map(
        local,
        mesh=mesh,
        in_specs=(
            P("row", "req", None),
            P("row", None),
            P(),
            P(None, None, "req"),
            P("req", None),
            P(),
            P(None, "req"),
            P("req", None),
            P(),
            P(("req", "row"), None),
            P("row", "req"),
        ),
        out_specs=P(("req", "row"), None),
        check_vma=False,
    )
```

profile of v0, /device:TPU:0, one launch (start us, length us, event | category | flops | bytes accessed | tf_op | source)
XLA Modules:
  0.0 349.8 jit_solution(17088282344082328541)
XLA Ops:
  6.5 1.2 convert_reduce_fusion.1
  7.7 1.2 fusion.59
  8.9 1.9 fusion.61
  11.5 1.4 reduce.7
  12.9 56.8 %all-gather.3.cloned.1.call-done = bf16[2048,1280]{1,0:T(8,128)(2,1)} async-done(((bf16[128,1280]{1,0:T(8,128)(2,1)}), bf16[2048,1280]{1,0:T(8,128)(2,1)}) %all-gather.3.cloned.1.call-update) | async-done | bytes 5242896 | tf_op jit(solution)/shard_map/all_gather | solution.py:41
  69.8 4.2 %fusion.105 = f32[2048,240]{0,1:S(1)} fusion(bf16[2048,1280]{1,0:T(8,128)(2,1)} %all-gather.3.cloned.1.call-done, bf16[1280,240]{0,1:T(8,128)(2,1)} %bitcast.94), kind=kOutput, calls=%fused_computation.160 | convolution fusion | flops 1258291200 | bytes 7823360
  75.0 11.0 %while.10 = (s32[]{:T(128)}, bf16[4,512,80]{1,2,0:T(8,128)(2,1)S(1)}, s32[4,512]{1,0:T(4,128)S(1)}, s32[1,2048]{1,0:T(1,128)S(1)}, bf16[4,512,80]{2,1,0:T(8,128)...) while((s32[]{:T(128)}, bf16[4,512,80]{1,2,0:T(8,128)(2,1)S(1)}, ...), condition=%wide.region_8.9_spmd, body=%wide.region_5.8_spmd.sunk | while | flops 345021440 | bytes 13869153 | solution.py:64
  75.1 0.9 fusion.125
  76.7 1.1 fusion.127
  79.4 1.1 fusion.127
  82.2 1.1 fusion.127
  84.9 1.1 fusion.127
  86.1 3.9 %convolution_convert_fusion.1 = bf16[2048,1280]{1,0:T(8,128)(2,1)} fusion(bf16[2048,80]{0,1:T(8,128)(2,1)S(1)} %bitcast.88, bf16[80,1280]{1,0:T(8,128)(2,1)S(1)} %copy-done.3), kind=kOutput, calls=%fused_computation.13 | convolution fusion | flops 422051840 | bytes 5775360 | tf_op jit(solution)/shard_map/dot_general | solution.py:70
  90.0 78.7 %reduce-scatter.3.cloned.1.call-done = bf16[128,1280]{1,0:T(8,128)(2,1)} async-done(((bf16[2048,1280]{1,0:T(8,128)(2,1)}), bf16[128,1280]{1,0:T(8,128)(2,1)}) %reduce-scatter.3.cloned.1.call-update) | async-done | bytes 327696 | tf_op jit(solution)/shard_map/reduce_scatter | solution.py:69
  168.8 1.2 convert_reduce_fusion
  170.2 1.0 fusion.58
  171.4 55.5 %all-gather.5.cloned.1.call-done = bf16[2048,1280]{1,0:T(8,128)(2,1)} async-done(((bf16[128,1280]{1,0:T(8,128)(2,1)}), bf16[2048,1280]{1,0:T(8,128)(2,1)}) %all-gather.5.cloned.1.call-update) | async-done | bytes 5242896 | tf_op jit(solution)/shard_map/all_gather | solution.py:79
  226.9 13.4 %convolution_convert_fusion = bf16[2048,1280]{1,0:T(8,128)(2,1)} fusion(bf16[320,1280]{1,0:T(8,128)(2,1)S(1)} %copy-done, bf16[2048,1280]{1,0:T(8,128)(2,1)} %all-gather.5.cloned.1.call-done, bf16[1280,320]{0,1:T(8,128)(2,1)S(1)} %copy-done.6), kind=kOutput, calls=%fused_computation.12 | convolution fusion | flops 3400663040 | bytes 12124160 | tf_op jit(solution)/shard_map/dot_general | solution.py:87
  242.0 5.3 %all-to-all-start = ((s32[16,1,2]{2,1,0:T(1,128)}), s32[16,1,2]{2,1,0:T(1,128)S(1)}, u32[]{:S(2)}, u32[]{:S(2)}) async-start(s32[16,1,2]{2,1,0:T(1,128)} %bitcast.9), calls=%async_computation | async-start | bytes 16384 | tf_op jit(solution)/shard_map/all_to_all | solution.py:115
  247.3 71.8 %reduce-scatter.5.cloned.1.call-done = bf16[128,1280]{1,0:T(8,128)(2,1)} async-done(((bf16[2048,1280]{1,0:T(8,128)(2,1)}), bf16[128,1280]{1,0:T(8,128)(2,1)}) %reduce-scatter.5.cloned.1.call-update) | async-done | bytes 327696 | tf_op jit(solution)/shard_map/reduce_scatter | solution.py:86
  319.1 1.0 fusion.63
  321.4 4.9 %all-to-all-start.1 = ((bf16[16,2,5120]{2,1,0:T(2,128)(2,1)}), bf16[16,2,5120]{2,1,0:T(2,128)(2,1)S(1)}, u32[]{:S(2)}, u32[]{:S(2)}) async-start(bf16[16,2,5120]{2,1,0:T(2,128)(2,1)} %reshape.113), calls=%async_computation.3 | async-start | bytes 655360 | tf_op jit(solution)/shard_map/all_to_all | solution.py:108
  327.2 7.9 %all-to-all-done.1 = bf16[16,2,5120]{2,1,0:T(2,128)(2,1)S(1)} async-done(((bf16[16,2,5120]{2,1,0:T(2,128)(2,1)}), bf16[16,2,5120]{2,1,0:T(2,128)(2,1)S(1)}, u32[]{:S(2)}, u32[]{:S(2)}) %all-to-all-start.1) | async-done | bytes 327712 | tf_op jit(solution)/shard_map/all_to_all | solution.py:108
  335.3 8.0 %fusion.18 = bf16[128,1280]{1,0:T(8,128)(2,1)} fusion(bf16[128,1280]{1,0:T(8,128)(2,1)S(1)} %copy-done.2, bf16[32,5120]{1,0:T(8,128)(2,1)S(1)} %reshape.114, bf16[5120,1280]{1,0:T(8,128)(2,1)} %param.21, pred[128]{0:T(512)(128)(4,1)S(1)} %fusion.64, s32[32]{0:T(128)S(1)} %eq.69), kind=kOutput, calls=%fused_computation.35 | convolution fusion | flops 430288896 | bytes 14090496 | tf_op jit(solution)/shard_map/dot_general | solution.py:123
  (64 shorter events, 11.8 us)
Async XLA Ops:
  6.5 220.4 %copy-start = (bf16[320,1280]{1,0:T(8,128)(2,1)S(1)}, bf16[320,1280]{1,0:T(8,128)(2,1)}, u32[]{:S(2)}) copy-start(bf16[320,1280]{1,0:T(8,128)(2,1)} %param.20) | copy-start | bytes 2457604
  6.5 63.2 %all-gather.3.cloned.1.call-start = ((), (), s32[]{:S(2)}) async-start(), calls=%async_computation.4 | async-start | bytes 5570560 | tf_op jit(solution)/shard_map/all_gather | solution.py:41
  10.9 157.9 %reduce-scatter.3.cloned.1.call-start = ((), (), s32[]{:S(2)}) async-start(), calls=%async_computation.5 | async-start | bytes 5570560 | tf_op jit(solution)/shard_map/reduce_scatter | solution.py:69
  74.1 0.9 copy-start.4
  75.0 11.0 %copy-start.3 = (bf16[80,1280]{1,0:T(8,128)(2,1)S(1)}, bf16[80,1280]{1,0:T(8,128)(2,1)}, u32[]{:S(2)}) copy-start(bf16[80,1280]{1,0:T(8,128)(2,1)} %param.17) | copy-start | bytes 614404
  90.0 78.8 %copy-start.1 = (bf16[1,128,1280]{2,1,0:T(8,128)(2,1)S(1)}, bf16[1,128,1280]{2,1,0:T(8,128)(2,1)}, u32[]{:S(2)}) copy-start(bf16[1,128,1280]{2,1,0:T(8,128)(2,1)} %param.13) | copy-start | bytes 983044
  90.0 80.2 %copy-start.5 = (f32[1280]{0:T(1024)S(1)}, f32[1280]{0:T(1024)}, u32[]{:S(2)}) copy-start(f32[1280]{0:T(1024)} %param.18) | copy-start | bytes 15364
  90.0 137.0 %copy-start.6 = (bf16[1280,320]{0,1:T(8,128)(2,1)S(1)}, bf16[1280,320]{0,1:T(8,128)(2,1)}, u32[]{:S(2)}) copy-start(bf16[1280,320]{0,1:T(8,128)(2,1)} %param.19) | copy-start | bytes 2457604
  90.0 136.9 %all-gather.5.cloned.1.call-start = ((), (), s32[]{:S(2)}) async-start(), calls=%async_computation.6 | async-start | bytes 5570560 | tf_op jit(solution)/shard_map/all_gather | solution.py:79
  171.2 147.9 %reduce-scatter.5.cloned.1.call-start = ((), (), s32[]{:S(2)}) async-start(), calls=%async_computation.7 | async-start | bytes 5570560 | tf_op jit(solution)/shard_map/reduce_scatter | solution.py:86
  240.3 0.7 copy-start.7
  241.0 94.3 %copy-start.2 = (bf16[128,1280]{1,0:T(8,128)(2,1)S(1)}, bf16[128,1280]{1,0:T(8,128)(2,1)}, u32[]{:S(2)}) copy-start(bf16[128,1280]{1,0:T(8,128)(2,1)} %param.22) | copy-start | bytes 983044
  242.0 79.4 %all-to-all-start = ((s32[16,1,2]{2,1,0:T(1,128)}), s32[16,1,2]{2,1,0:T(1,128)S(1)}, u32[]{:S(2)}, u32[]{:S(2)}) async-start(s32[16,1,2]{2,1,0:T(1,128)} %bitcast.9), calls=%async_computation | async-start | bytes 16384 | tf_op jit(solution)/shard_map/all_to_all | solution.py:115
  321.4 13.8 %all-to-all-start.1 = ((bf16[16,2,5120]{2,1,0:T(2,128)(2,1)}), bf16[16,2,5120]{2,1,0:T(2,128)(2,1)S(1)}, u32[]{:S(2)}, u32[]{:S(2)}) async-start(bf16[16,2,5120]{2,1,0:T(2,128)(2,1)} %reshape.113), calls=%async_computation.3 | async-start | bytes 655360 | tf_op jit(solution)/shard_map/all_to_all | solution.py:108
Sparse Core Ops, SparseCore 0:
  11.0 58.7 all-gather.2
  90.1 78.6 reduce-scatter.2
  171.3 55.5 all-gather.4
  240.5 78.5 reduce-scatter.4
where the time goes:
time: 350 us
  waiting for transfers between devices  271 us (77%)
  matrix products  37.6 us (11%)
  between operations  13.3 us (4%)
  other arithmetic  13.2 us (4%)
  starting transfers between devices  10.5 us (3%)
  local copies, waits for them, and re-layouts  4.15 us (1%)
    reduce_scatter x1, waiting for transfers between devices, local(): lax.psum_scatter(jnp.dot(piece, w_out, preferred_element_type=jnp.float32...  78.7 us
    reduce_scatter x1, waiting for transfers between devices, local(): lax.psum_scatter(jnp.dot(piece, w_down, preferred_element_type=jnp.float3...  71.8 us
    all_gather x1, waiting for transfers between devices, local(): lax.all_gather(normed, 'req', axis=0, tiled=True)  56.8 us
    all_gather x1, waiting for transfers between devices, local(): lax.all_gather(normed_two, 'req', axis=0, tiled=True)  55.5 us
    dot_general x1, matrix products, local(): jnp.dot(piece, w_down, preferred_element_type=jnp.float32)  13.4 us
    dot_general x1, matrix products, local(): jnp.dot(placer.astype(jnp.bfloat16), incoming, preferred_element_type=jnp...  7.96 us
    all_to_all x1, waiting for transfers between devices, local(): lax.all_to_all(outgoing.reshape(req_count, slot_cap, -1), 'req', split_ax...  7.94 us
  transfers between devices with their start and end apart: 6, of which 5 were waited for; matrix products, arithmetic and copies ran while one was open for 2% of the time, Pallas kernels for 0%

commit v1 on v0

--- a/solution.py
+++ b/solution.py
@@ -5,6 +5,28 @@
 from jax.sharding import PartitionSpec as P
 
 HEAD = 80
+
+
+def joined_along(parts, dim):
+    lengths = list(parts.shape[1:])
+    lengths[dim] *= parts.shape[0]
+    return jnp.moveaxis(parts, 0, dim).reshape(lengths)
+
+
+def ring_gather(array, axis, dim):
+    size = lax.axis_size(axis)
+    pairs = [(i, (i + 1) % size) for i in range(size)]
+    back = [(b, a) for a, b in pairs]
+    lower, upper = ([], [])
+    for lap in range(size - 1):
+        if lap % 2 == 0:
+            lower.append(lax.ppermute(lower[-1] if lower else array, axis, pairs))
+        else:
+            upper.append(lax.ppermute(upper[-1] if upper else array, axis, back))
+    tiles = jnp.stack([*lower[::-1], array, *upper])
+    shift = lax.axis_index(axis) - len(lower)
+    tiles = tiles[(jnp.arange(size) - shift) % size]
+    return joined_along(tiles, dim)
 
 
 def layer_norm(rows, gain):
@@ -75,11 +97,7 @@
     resid = (rows.astype(jnp.float32) + attn).astype(jnp.bfloat16)
     normed_two = layer_norm(resid, ln_mlp).astype(jnp.bfloat16)
     hidden = jax.nn.gelu(
-        jnp.dot(
-            lax.all_gather(normed_two, "req", axis=0, tiled=True),
-            w_up,
-            preferred_element_type=jnp.float32,
-        ),
+        jnp.dot(ring_gather(normed_two, "req", 0), w_up, preferred_element_type=jnp.float32),
         approximate=False,
     ).astype(jnp.bfloat16)
     piece = lax.slice_in_dim(hidden, 0, local_rows * lax.axis_size("req"), axis=0)

time: 350 us -> 404 us (1.15)
  starting transfers between devices: 10.5 us -> 48.2 us
  local copies, waits for them, and re-layouts: 4.15 us -> 27 us
  waiting for transfers between devices: 271 us -> 264 us
    all_gather x1 -> x0, waiting for transfers between devices: 55.5 us -> none  [local(): lax.all_gather(normed_two, 'req', axis=0, tiled=True)]
    ppermute x0 -> x15, waiting for transfers between devices: none -> 50.1 us  [the longest x8 49.7 us: ring_gather(): lower.append(lax.ppermute(lower[-1] if lower else array, axis, pairs))]
    ppermute x0 -> x15, starting transfers between devices: none -> 39.8 us  [the longest x7 38.5 us: ring_gather(): upper.append(lax.ppermute(upper[-1] if upper else array, axis, back))]
    unnamed x17 -> x39, local copies, waits for them, and re-layouts: 1.24 us -> 17.5 us
    gather x0 -> x1, local copies, waits for them, and re-layouts: none -> 5.78 us  [ring_gather(): tiles = tiles[(jnp.arange(size) - shift) % size]]
  transfers between devices with their start and end apart: 6 -> 20, of which waited for: 5 -> 13; matrix products, arithmetic and copies ran while one was open for 2% -> 6% of each run, Pallas kernels for 0% -> 0%
where the time goes in v1:
time: 404 us
  waiting for transfers between devices  264 us (65%)
  starting transfers between devices  48.2 us (12%)
  matrix products  37.5 us (9%)
  local copies, waits for them, and re-layouts  27 us (7%)
  between operations  13.4 us (3%)
  other arithmetic  13.3 us (3%)
    reduce_scatter x1, waiting for transfers between devices, local(): lax.psum_scatter(jnp.dot(piece, w_out, preferred_element_type=jnp.float32...  78.7 us
    reduce_scatter x1, waiting for transfers between devices, local(): lax.psum_scatter(jnp.dot(piece, w_down, preferred_element_type=jnp.float3...  70.3 us
    all_gather x1, waiting for transfers between devices, local(): lax.all_gather(normed, 'req', axis=0, tiled=True)  57 us
    ppermute x8, waiting for transfers between devices, ring_gather(): lower.append(lax.ppermute(lower[-1] if lower else array, axis, pairs))  49.7 us
    ppermute x7, starting transfers between devices, ring_gather(): upper.append(lax.ppermute(upper[-1] if upper else array, axis, back))  38.5 us
    unnamed x39, local copies, waits for them, and re-layouts  17.5 us
    dot_general x1, matrix products, local(): jnp.dot(piece, w_down, preferred_element_type=jnp.float32)  13.4 us
  transfers between devices with their start and end apart: 20, of which 13 were waited for; matrix products, arithmetic and copies ran while one was open for 6% of the time, Pallas kernels for 0%

profile of v1, /device:TPU:0, one launch (start us, length us, event | category | flops | bytes accessed | tf_op | source)
XLA Modules:
  0.0 403.7 jit_solution(7856017601669914221)
XLA Ops:
  12.8 57.0 %all-gather.2.cloned.1.call-done = bf16[2048,1280]{1,0:T(8,128)(2,1)} async-done(((bf16[128,1280]{1,0:T(8,128)(2,1)}), bf16[2048,1280]{1,0:T(8,128)(2,1)}) %all-gather.2.cloned.1.call-update) | async-done | bytes 5242896 | tf_op jit(solution)/shard_map/all_gather | solution.py:63
  75.0 10.9 %while.10 = (s32[]{:T(128)}, bf16[4,512,80]{1,2,0:T(8,128)(2,1)S(1)}, s32[4,512]{1,0:T(4,128)S(1)}, s32[1,2048]{1,0:T(1,128)S(1)}, bf16[4,512,80]{2,1,0:T(8,128)...) while((s32[]{:T(128)}, bf16[4,512,80]{1,2,0:T(8,128)(2,1)S(1)}, ...), condition=%wide.region_8.9_spmd, body=%wide.region_5.8_spmd.sunk | while | flops 345021440 | bytes 13869153 | solution.py:86
  90.0 78.7 %reduce-scatter.3.cloned.1.call-done = bf16[128,1280]{1,0:T(8,128)(2,1)} async-done(((bf16[2048,1280]{1,0:T(8,128)(2,1)}), bf16[128,1280]{1,0:T(8,128)(2,1)}) %reduce-scatter.3.cloned.1.call-update) | async-done | bytes 327696 | tf_op jit(solution)/shard_map/reduce_scatter | solution.py:91
  171.7 10.5 %collective-permute-done = bf16[128,1280]{1,0:T(8,128)(2,1)S(1)} collective-permute-done((bf16[128,1280]{1,0:T(8,128)(2,1)S(1)}, bf16[128,1280]{1,0:T(8,128)(2,1)S(1)}, u32[]{:S(2)}, u32[]{:S(2)}) %collective-permute-start) | collective-permute-done | bytes 327712 | tf_op jit(solution)/shard_map/ppermute | solution.py:23
  182.2 5.3 %collective-permute-start.8 = (bf16[128,1280]{1,0:T(8,128)(2,1)S(1)}, bf16[128,1280]{1,0:T(8,128)(2,1)S(1)}, u32[]{:S(2)}, u32[]{:S(2)}) collective-permute-start(bf16[128,1280]{1,0:T(8,128)(2,1)S(1)} %fusion.58), channel_id=1, source_target_pairs={{8,0},{16,8},{24,16},{32,24},{40,32},{48,40},{56,48},{64,56},{72,6... | collective-permute-start | bytes 983048 | tf_op jit(solution)/shard_map/ppermute | solution.py:25
  187.5 5.4 %collective-permute-done.1 = bf16[128,1280]{1,0:T(8,128)(2,1)S(1)} collective-permute-done((bf16[128,1280]{1,0:T(8,128)(2,1)S(1)}, bf16[128,1280]{1,0:T(8,128)(2,1)S(1)}, u32[]{:S(2)}, u32[]{:S(2)}) %collective-permute-start.1) | collective-permute-done | bytes 327712 | tf_op jit(solution)/shard_map/ppermute | solution.py:23
  192.9 5.3 %collective-permute-start.9 = (bf16[128,1280]{1,0:T(8,128)(2,1)S(1)}, bf16[128,1280]{1,0:T(8,128)(2,1)S(1)}, u32[]{:S(2)}, u32[]{:S(2)}) collective-permute-start(bf16[128,1280]{1,0:T(8,128)(2,1)S(1)} %collective-permute-done.8), channel_id=1, source_target_pairs={{8,0},{16,8},{24,16},{32,24},{40,32},{48,40},{56,48},{64,56},{72,6... | collective-permute-start | bytes 983048 | tf_op jit(solution)/shard_map/ppermute | solution.py:25
  198.3 5.0 %collective-permute-done.2 = bf16[128,1280]{1,0:T(8,128)(2,1)S(1)} collective-permute-done((bf16[128,1280]{1,0:T(8,128)(2,1)S(1)}, bf16[128,1280]{1,0:T(8,128)(2,1)S(1)}, u32[]{:S(2)}, u32[]{:S(2)}) %collective-permute-start.2) | collective-permute-done | bytes 327712 | tf_op jit(solution)/shard_map/ppermute | solution.py:23
  203.3 5.3 %collective-permute-start.10 = (bf16[128,1280]{1,0:T(8,128)(2,1)S(1)}, bf16[128,1280]{1,0:T(8,128)(2,1)S(1)}, u32[]{:S(2)}, u32[]{:S(2)}) collective-permute-start(bf16[128,1280]{1,0:T(8,128)(2,1)S(1)} %collective-permute-done.9), channel_id=1, source_target_pairs={{8,0},{16,8},{24,16},{32,24},{40,32},{48,40},{56,48},{64,56},{72,6... | collective-permute-start | bytes 983048 | tf_op jit(solution)/shard_map/ppermute | solution.py:25
  208.7 5.0 %collective-permute-done.3 = bf16[128,1280]{1,0:T(8,128)(2,1)S(1)} collective-permute-done((bf16[128,1280]{1,0:T(8,128)(2,1)S(1)}, bf16[128,1280]{1,0:T(8,128)(2,1)S(1)}, u32[]{:S(2)}, u32[]{:S(2)}) %collective-permute-start.3) | collective-permute-done | bytes 327712 | tf_op jit(solution)/shard_map/ppermute | solution.py:23
  213.7 5.3 %collective-permute-start.11 = (bf16[128,1280]{1,0:T(8,128)(2,1)S(1)}, bf16[128,1280]{1,0:T(8,128)(2,1)S(1)}, u32[]{:S(2)}, u32[]{:S(2)}) collective-permute-start(bf16[128,1280]{1,0:T(8,128)(2,1)S(1)} %collective-permute-done.10), channel_id=1, source_target_pairs={{8,0},{16,8},{24,16},{32,24},{40,32},{48,40},{56,48},{64,56},{72,6... | collective-permute-start | bytes 983048 | tf_op jit(solution)/shard_map/ppermute | solution.py:25
  219.1 5.6 %collective-permute-done.4 = bf16[128,1280]{1,0:T(8,128)(2,1)S(1)} collective-permute-done((bf16[128,1280]{1,0:T(8,128)(2,1)S(1)}, bf16[128,1280]{1,0:T(8,128)(2,1)S(1)}, u32[]{:S(2)}, u32[]{:S(2)}) %collective-permute-start.4) | collective-permute-done | bytes 327712 | tf_op jit(solution)/shard_map/ppermute | solution.py:23
  224.7 5.6 %collective-permute-start.12 = (bf16[128,1280]{1,0:T(8,128)(2,1)S(1)}, bf16[128,1280]{1,0:T(8,128)(2,1)}, u32[]{:S(2)}, u32[]{:S(2)}) collective-permute-start(bf16[128,1280]{1,0:T(8,128)(2,1)S(1)} %collective-permute-done.11), channel_id=1, source_target_pairs={{8,0},{16,8},{24,16},{32,24},{40,32},{48,40},{56,48},{64,56},{72,6... | collective-permute-start | bytes 983048 | tf_op jit(solution)/shard_map/ppermute | solution.py:25
  230.3 6.4 %collective-permute-done.5 = bf16[128,1280]{1,0:T(8,128)(2,1)S(1)} collective-permute-done((bf16[128,1280]{1,0:T(8,128)(2,1)S(1)}, bf16[128,1280]{1,0:T(8,128)(2,1)S(1)}, u32[]{:S(2)}, u32[]{:S(2)}) %collective-permute-start.5) | collective-permute-done | bytes 327712 | tf_op jit(solution)/shard_map/ppermute | solution.py:23
  236.7 5.7 %collective-permute-start.13 = (bf16[128,1280]{1,0:T(8,128)(2,1)}, bf16[128,1280]{1,0:T(8,128)(2,1)}, u32[]{:S(2)}, u32[]{:S(2)}) collective-permute-start(bf16[128,1280]{1,0:T(8,128)(2,1)} %collective-permute-done.12), channel_id=1, source_target_pairs={{8,0},{16,8},{24,16},{32,24},{40,32},{48,40},{56,48},{64,56},{72,6... | collective-permute-start | bytes 983048 | tf_op jit(solution)/shard_map/ppermute | solution.py:25
  242.4 7.2 %collective-permute-done.6 = bf16[128,1280]{1,0:T(8,128)(2,1)} collective-permute-done((bf16[128,1280]{1,0:T(8,128)(2,1)S(1)}, bf16[128,1280]{1,0:T(8,128)(2,1)}, u32[]{:S(2)}, u32[]{:S(2)}) %collective-permute-start.6) | collective-permute-done | bytes 327712 | tf_op jit(solution)/shard_map/ppermute | solution.py:23
  250.1 5.8 %collective-permute-start.14 = (bf16[128,1280]{1,0:T(8,128)(2,1)}, bf16[128,1280]{1,0:T(8,128)(2,1)S(1)}, u32[]{:S(2)}, u32[]{:S(2)}) collective-permute-start(bf16[128,1280]{1,0:T(8,128)(2,1)} %collective-permute-done.13), channel_id=1, source_target_pairs={{8,0},{16,8},{24,16},{32,24},{40,32},{48,40},{56,48},{64,56},{72,6... | collective-permute-start | bytes 983048 | tf_op jit(solution)/shard_map/ppermute | solution.py:25
  255.9 4.5 %collective-permute-done.7 = bf16[128,1280]{1,0:T(8,128)(2,1)} collective-permute-done((bf16[128,1280]{1,0:T(8,128)(2,1)}, bf16[128,1280]{1,0:T(8,128)(2,1)}, u32[]{:S(2)}, u32[]{:S(2)}) %collective-permute-start.7) | collective-permute-done | bytes 327712 | tf_op jit(solution)/shard_map/ppermute | solution.py:23
  278.4 5.8 %gather_fusion = bf16[16,128,1280]{2,1,0:T(8,128)(2,1)} fusion(bf16[16,128,1280]{2,1,0:T(8,128)(2,1)} %bitcast_dynamic-update-slice_fusion, s32[1024]{0:T(1024)S(1)} %pad_clamp_fusion), kind=kCustom, calls=%fused_computation | custom fusion | bytes 10485824 | tf_op jit(solution)/shard_map/gather | solution.py:28
  284.2 13.4 %convolution_convert_fusion = bf16[2048,1280]{1,0:T(8,128)(2,1)} fusion(bf16[320,1280]{1,0:T(8,128)(2,1)S(1)} %copy-done, bf16[2048,1280]{1,0:T(8,128)(2,1)} %bitcast.123, bf16[1280,320]{0,1:T(8,128)(2,1)S(1)} %copy-done.10), kind=kOutput, calls=%fused_computation.13 | convolution fusion | flops 3400663040 | bytes 12124160 | tf_op jit(solution)/shard_map/dot_general | solution.py:105
  302.7 70.3 %reduce-scatter.5.cloned.1.call-done = bf16[128,1280]{1,0:T(8,128)(2,1)} async-done(((bf16[2048,1280]{1,0:T(8,128)(2,1)}), bf16[128,1280]{1,0:T(8,128)(2,1)}) %reduce-scatter.5.cloned.1.call-update) | async-done | bytes 327696 | tf_op jit(solution)/shard_map/reduce_scatter | solution.py:104
  375.3 4.9 %all-to-all-start.1 = ((bf16[16,2,5120]{2,1,0:T(2,128)(2,1)}), bf16[16,2,5120]{2,1,0:T(2,128)(2,1)S(1)}, u32[]{:S(2)}, u32[]{:S(2)}) async-start(bf16[16,2,5120]{2,1,0:T(2,128)(2,1)} %reshape.166), calls=%async_computation.3 | async-start | bytes 655360 | tf_op jit(solution)/shard_map/all_to_all | solution.py:126
  381.0 8.1 %all-to-all-done.1 = bf16[16,2,5120]{2,1,0:T(2,128)(2,1)S(1)} async-done(((bf16[16,2,5120]{2,1,0:T(2,128)(2,1)}), bf16[16,2,5120]{2,1,0:T(2,128)(2,1)S(1)}, u32[]{:S(2)}, u32[]{:S(2)}) %all-to-all-start.1) | async-done | bytes 327712 | tf_op jit(solution)/shard_map/all_to_all | solution.py:126
  389.2 7.9 %fusion.18 = bf16[128,1280]{1,0:T(8,128)(2,1)} fusion(bf16[128,1280]{1,0:T(8,128)(2,1)S(1)} %copy-done.2, bf16[32,5120]{1,0:T(8,128)(2,1)S(1)} %reshape.167, bf16[5120,1280]{1,0:T(8,128)(2,1)} %param.21, pred[128]{0:T(512)(128)(4,1)S(1)} %fusion.64, s32[32]{0:T(128)S(1)} %eq.71), kind=kOutput, calls=%fused_computation.36 | convolution fusion | flops 430288896 | bytes 14090496 | tf_op jit(solution)/shard_map/dot_general | solution.py:141
  (118 shorter events, 56.0 us)
Async XLA Ops:
  6.5 277.7 %copy-start = (bf16[320,1280]{1,0:T(8,128)(2,1)S(1)}, bf16[320,1280]{1,0:T(8,128)(2,1)}, u32[]{:S(2)}) copy-start(bf16[320,1280]{1,0:T(8,128)(2,1)} %param.20) | copy-start | bytes 2457604
  6.5 63.2 %all-gather.2.cloned.1.call-start = ((), (), s32[]{:S(2)}) async-start(), calls=%async_computation.4 | async-start | bytes 5570560 | tf_op jit(solution)/shard_map/all_gather | solution.py:63
  10.9 157.8 %reduce-scatter.3.cloned.1.call-start = ((), (), s32[]{:S(2)}) async-start(), calls=%async_computation.5 | async-start | bytes 5570560 | tf_op jit(solution)/shard_map/reduce_scatter | solution.py:91
  89.9 78.8 %copy-start.1 = (bf16[1,128,1280]{2,1,0:T(8,128)(2,1)S(1)}, bf16[1,128,1280]{2,1,0:T(8,128)(2,1)}, u32[]{:S(2)}) copy-start(bf16[1,128,1280]{2,1,0:T(8,128)(2,1)} %param.13) | copy-start | bytes 983044
  89.9 80.2 %copy-start.8 = (f32[1280]{0:T(1024)S(1)}, f32[1280]{0:T(1024)}, u32[]{:S(2)}) copy-start(f32[1280]{0:T(1024)} %param.18) | copy-start | bytes 15364
  89.9 283.1 %reduce-scatter.5.cloned.1.call-start = ((), (), s32[]{:S(2)}) async-start(), calls=%async_computation.6 | async-start | bytes 5570560 | tf_op jit(solution)/shard_map/reduce_scatter | solution.py:104
  170.4 11.8 %collective-permute-start = (bf16[128,1280]{1,0:T(8,128)(2,1)S(1)}, bf16[128,1280]{1,0:T(8,128)(2,1)S(1)}, u32[]{:S(2)}, u32[]{:S(2)}) collective-permute-start(bf16[128,1280]{1,0:T(8,128)(2,1)S(1)} %fusion.58), channel_id=1, source_target_pairs={{0,8},{8,16},{16,24},{24,32},{32,40},{40,48},{48,56},{56,64},{64,7... | collective-permute-start | bytes 983048 | tf_op jit(solution)/shard_map/ppermute | solution.py:23
  182.2 10.8 %collective-permute-start.1 = (bf16[128,1280]{1,0:T(8,128)(2,1)S(1)}, bf16[128,1280]{1,0:T(8,128)(2,1)S(1)}, u32[]{:S(2)}, u32[]{:S(2)}) collective-permute-start(bf16[128,1280]{1,0:T(8,128)(2,1)S(1)} %collective-permute-done), channel_id=1, source_target_pairs={{0,8},{8,16},{16,24},{24,32},{32,40},{40,48},{48,56},{56,64},{64,7... | collective-permute-start | bytes 983048 | tf_op jit(solution)/shard_map/ppermute | solution.py:23
  182.2 10.8 %collective-permute-start.8 = (bf16[128,1280]{1,0:T(8,128)(2,1)S(1)}, bf16[128,1280]{1,0:T(8,128)(2,1)S(1)}, u32[]{:S(2)}, u32[]{:S(2)}) collective-permute-start(bf16[128,1280]{1,0:T(8,128)(2,1)S(1)} %fusion.58), channel_id=1, source_target_pairs={{8,0},{16,8},{24,16},{32,24},{40,32},{48,40},{56,48},{64,56},{72,6... | collective-permute-start | bytes 983048 | tf_op jit(solution)/shard_map/ppermute | solution.py:25
  192.9 10.4 %collective-permute-start.2 = (bf16[128,1280]{1,0:T(8,128)(2,1)S(1)}, bf16[128,1280]{1,0:T(8,128)(2,1)S(1)}, u32[]{:S(2)}, u32[]{:S(2)}) collective-permute-start(bf16[128,1280]{1,0:T(8,128)(2,1)S(1)} %collective-permute-done.1), channel_id=1, source_target_pairs={{0,8},{8,16},{16,24},{24,32},{32,40},{40,48},{48,56},{56,64},{64,7... | collective-permute-start | bytes 983048 | tf_op jit(solution)/shard_map/ppermute | solution.py:23
  192.9 10.4 %collective-permute-start.9 = (bf16[128,1280]{1,0:T(8,128)(2,1)S(1)}, bf16[128,1280]{1,0:T(8,128)(2,1)S(1)}, u32[]{:S(2)}, u32[]{:S(2)}) collective-permute-start(bf16[128,1280]{1,0:T(8,128)(2,1)S(1)} %collective-permute-done.8), channel_id=1, source_target_pairs={{8,0},{16,8},{24,16},{32,24},{40,32},{48,40},{56,48},{64,56},{72,6... | collective-permute-start | bytes 983048 | tf_op jit(solution)/shard_map/ppermute | solution.py:25
  203.3 10.4 %collective-permute-start.3 = (bf16[128,1280]{1,0:T(8,128)(2,1)S(1)}, bf16[128,1280]{1,0:T(8,128)(2,1)S(1)}, u32[]{:S(2)}, u32[]{:S(2)}) collective-permute-start(bf16[128,1280]{1,0:T(8,128)(2,1)S(1)} %collective-permute-done.2), channel_id=1, source_target_pairs={{0,8},{8,16},{16,24},{24,32},{32,40},{40,48},{48,56},{56,64},{64,7... | collective-permute-start | bytes 983048 | tf_op jit(solution)/shard_map/ppermute | solution.py:23
  203.3 10.4 %collective-permute-start.10 = (bf16[128,1280]{1,0:T(8,128)(2,1)S(1)}, bf16[128,1280]{1,0:T(8,128)(2,1)S(1)}, u32[]{:S(2)}, u32[]{:S(2)}) collective-permute-start(bf16[128,1280]{1,0:T(8,128)(2,1)S(1)} %collective-permute-done.9), channel_id=1, source_target_pairs={{8,0},{16,8},{24,16},{32,24},{40,32},{48,40},{56,48},{64,56},{72,6... | collective-permute-start | bytes 983048 | tf_op jit(solution)/shard_map/ppermute | solution.py:25
  213.7 10.9 %collective-permute-start.4 = (bf16[128,1280]{1,0:T(8,128)(2,1)S(1)}, bf16[128,1280]{1,0:T(8,128)(2,1)S(1)}, u32[]{:S(2)}, u32[]{:S(2)}) collective-permute-start(bf16[128,1280]{1,0:T(8,128)(2,1)S(1)} %collective-permute-done.3), channel_id=1, source_target_pairs={{0,8},{8,16},{16,24},{24,32},{32,40},{40,48},{48,56},{56,64},{64,7... | collective-permute-start | bytes 983048 | tf_op jit(solution)/shard_map/ppermute | solution.py:23
  213.7 10.9 %collective-permute-start.11 = (bf16[128,1280]{1,0:T(8,128)(2,1)S(1)}, bf16[128,1280]{1,0:T(8,128)(2,1)S(1)}, u32[]{:S(2)}, u32[]{:S(2)}) collective-permute-start(bf16[128,1280]{1,0:T(8,128)(2,1)S(1)} %collective-permute-done.10), channel_id=1, source_target_pairs={{8,0},{16,8},{24,16},{32,24},{40,32},{48,40},{56,48},{64,56},{72,6... | collective-permute-start | bytes 983048 | tf_op jit(solution)/shard_map/ppermute | solution.py:25
  224.7 12.0 %collective-permute-start.5 = (bf16[128,1280]{1,0:T(8,128)(2,1)S(1)}, bf16[128,1280]{1,0:T(8,128)(2,1)S(1)}, u32[]{:S(2)}, u32[]{:S(2)}) collective-permute-start(bf16[128,1280]{1,0:T(8,128)(2,1)S(1)} %collective-permute-done.4), channel_id=1, source_target_pairs={{0,8},{8,16},{16,24},{24,32},{32,40},{40,48},{48,56},{56,64},{64,7... | collective-permute-start | bytes 983048 | tf_op jit(solution)/shard_map/ppermute | solution.py:23
  224.7 12.0 %collective-permute-start.12 = (bf16[128,1280]{1,0:T(8,128)(2,1)S(1)}, bf16[128,1280]{1,0:T(8,128)(2,1)}, u32[]{:S(2)}, u32[]{:S(2)}) collective-permute-start(bf16[128,1280]{1,0:T(8,128)(2,1)S(1)} %collective-permute-done.11), channel_id=1, source_target_pairs={{8,0},{16,8},{24,16},{32,24},{40,32},{48,40},{56,48},{64,56},{72,6... | collective-permute-start | bytes 983048 | tf_op jit(solution)/shard_map/ppermute | solution.py:25
  236.7 12.9 %collective-permute-start.6 = (bf16[128,1280]{1,0:T(8,128)(2,1)S(1)}, bf16[128,1280]{1,0:T(8,128)(2,1)}, u32[]{:S(2)}, u32[]{:S(2)}) collective-permute-start(bf16[128,1280]{1,0:T(8,128)(2,1)S(1)} %collective-permute-done.5), channel_id=1, source_target_pairs={{0,8},{8,16},{16,24},{24,32},{32,40},{40,48},{48,56},{56,64},{64,7... | collective-permute-start | bytes 983048 | tf_op jit(solution)/shard_map/ppermute | solution.py:23
  236.7 13.4 %collective-permute-start.13 = (bf16[128,1280]{1,0:T(8,128)(2,1)}, bf16[128,1280]{1,0:T(8,128)(2,1)}, u32[]{:S(2)}, u32[]{:S(2)}) collective-permute-start(bf16[128,1280]{1,0:T(8,128)(2,1)} %collective-permute-done.12), channel_id=1, source_target_pairs={{8,0},{16,8},{24,16},{32,24},{40,32},{48,40},{56,48},{64,56},{72,6... | collective-permute-start | bytes 983048 | tf_op jit(solution)/shard_map/ppermute | solution.py:25
  249.6 10.7 %collective-permute-start.7 = (bf16[128,1280]{1,0:T(8,128)(2,1)}, bf16[128,1280]{1,0:T(8,128)(2,1)}, u32[]{:S(2)}, u32[]{:S(2)}) collective-permute-start(bf16[128,1280]{1,0:T(8,128)(2,1)} %collective-permute-done.6), channel_id=1, source_target_pairs={{0,8},{8,16},{16,24},{24,32},{32,40},{40,48},{48,56},{56,64},{64,7... | collective-permute-start | bytes 983048 | tf_op jit(solution)/shard_map/ppermute | solution.py:23
  250.1 27.6 %collective-permute-start.14 = (bf16[128,1280]{1,0:T(8,128)(2,1)}, bf16[128,1280]{1,0:T(8,128)(2,1)S(1)}, u32[]{:S(2)}, u32[]{:S(2)}) collective-permute-start(bf16[128,1280]{1,0:T(8,128)(2,1)} %collective-permute-done.13), channel_id=1, source_target_pairs={{8,0},{16,8},{24,16},{32,24},{40,32},{48,40},{56,48},{64,56},{72,6... | collective-permute-start | bytes 983048 | tf_op jit(solution)/shard_map/ppermute | solution.py:25
  298.2 91.0 %copy-start.2 = (bf16[128,1280]{1,0:T(8,128)(2,1)S(1)}, bf16[128,1280]{1,0:T(8,128)(2,1)}, u32[]{:S(2)}) copy-start(bf16[128,1280]{1,0:T(8,128)(2,1)} %param.22) | copy-start | bytes 983044
  299.3 76.1 %all-to-all-start = ((s32[16,1,2]{2,1,0:T(1,128)}), s32[16,1,2]{2,1,0:T(1,128)S(1)}, u32[]{:S(2)}, u32[]{:S(2)}) async-start(s32[16,1,2]{2,1,0:T(1,128)} %bitcast.9), calls=%async_computation | async-start | bytes 16384 | tf_op jit(solution)/shard_map/all_to_all | solution.py:133
  375.3 13.7 %all-to-all-start.1 = ((bf16[16,2,5120]{2,1,0:T(2,128)(2,1)}), bf16[16,2,5120]{2,1,0:T(2,128)(2,1)S(1)}, u32[]{:S(2)}, u32[]{:S(2)}) async-start(bf16[16,2,5120]{2,1,0:T(2,128)(2,1)} %reshape.166), calls=%async_computation.3 | async-start | bytes 655360 | tf_op jit(solution)/shard_map/all_to_all | solution.py:126
  (8 other events, 89.6 us)
Sparse Core Ops, SparseCore 0:
  11.0 58.7 all-gather.1
  90.0 78.6 reduce-scatter.2
  297.7 75.2 reduce-scatter.4
